TPU v7x, 32 devices: a whole 2x2x4 slice. The times are simulated.
32 devices in a mesh: depth: 4 (over z), imx: 4 (over y, x), imy: 2 (over core).
Axes of the slice: x: 2, y: 2, z: 4, core: 2. Of those that a mesh axis runs over, the one named last changes fastest.
Arguments:
- field: bfloat16 [128, 256, 512], P('depth', 'imy', 'imx'), may hold values from -6 to 6
- brick_live: int32 [4, 8, 16], P('depth', 'imy', 'imx'), may hold values from 0 to 1, as said below
- order: int32 [32, 64], P('imy', 'imx'), may hold values 0 or 1
- centers: float32 [4], replicated, may hold values from -2 to 2
- widths: float32 [4], replicated, may hold values from 0.3 to 1.2
- heights: float32 [4], replicated, may hold values from 0.5 to 3
- colours: float32 [4, 3], replicated, may hold values from 0.1 to 1
Outputs:
- colour: float32 [3, 256, 512], P(None, ('imy', 'depth'), 'imx')
- logtrans: float32 [256, 512], P(('imy', 'depth'), 'imx')
Inputs may be any that keep to these rules, and one draw needn't show every extreme that they name: `brick_live`: each device's 16 bricks (one slab, 4 bricks along the rows by 4 along the columns) hold between 1 and 16 live bricks; at least one device has all 16 live, and most have few.
All inputs are finite; a program needn't handle non-finite values. No bound on the sum of `order` on one device may be relied on, other than what follows from the above.
Results may differ from a plain program's by a relative error of at most 0.00038.
Values may be sent and summed in bfloat16 or wider, within the bound.
A program may use at most 64 MiB of HBM per device.

v0:
```python
import functools
import math

import jax
import jax.numpy as jnp
from jax import lax
from jax.experimental import pallas as pl
from jax.experimental.pallas import tpu as pltpu
from jax.sharding import PartitionSpec as P

OPTICAL = 3.0
MESH = pl.DeviceIdType.MESH
SUB = 8
PACK = 16
F32 = jnp.float32
BF16 = jnp.bfloat16
LEVELS = 32000.0
LOG2E = math.log2(math.e)


def iota(shape, dim):
    return lax.broadcasted_iota(jnp.int32, shape, dim)


def expand(small, rows, cols):
    high, wide = small.shape
    down = (iota((rows, high), 0) // (rows // high) == iota((rows, high), 1)).astype(F32).astype(BF16)
    along = (iota((wide, cols), 1) // (cols // wide) == iota((wide, cols), 0)).astype(F32).astype(BF16)
    tall = jnp.dot(down, small.astype(F32).astype(BF16), preferred_element_type=F32)
    return jnp.dot(tall.astype(BF16), along, preferred_element_type=F32)


def kernel(
    counts, step_len,
    field, live_in, order_in, centers_in, widths_in, heights_in, colours_in,
    colour_out, logt_out,
    fb, live, order, centers, widths, heights, colours,
    vf, zlo, zhi, xlo, xhi, face, flo, fhi, weights, lobes, scales, flag, logs, logs_in, tiles_out, tiles_in, gy, stage, peaks_out, peaks_in,
    load_sem, halo_send, halo_recv, log_send, log_recv, tile_send, tile_recv, peak_send, peak_recv,
):
    ndepth, nimx, nimy = counts
    me = lax.axis_index("depth")
    mx = lax.axis_index("imx")
    my = lax.axis_index("imy")
    zdev, xdev, ydev = fb.shape
    rows_out = xdev // ndepth
    nb = centers.shape[0]
    rows_blk = min(PACK, rows_out)

    pairs = ((field, fb), (order_in, order), (live_in, live), (centers_in, centers),
             (widths_in, widths), (heights_in, heights), (colours_in, colours))
    loads = [pltpu.make_async_copy(src, dst, load_sem.at[at]) for at, (src, dst) in enumerate(pairs)]
    for load in loads:
        load.start()

    barrier = pltpu.get_barrier_semaphore()
    for step in range(1, ndepth):
        pl.semaphore_signal(barrier, inc=1, device_id={"depth": lax.rem(me + step, ndepth)}, device_id_type=MESH)
    for axis, pos, count in (("imx", mx, nimx), ("imy", my, nimy)):
        @pl.when(pos > 0)
        def _():
            pl.semaphore_signal(barrier, inc=1, device_id={axis: pos - 1}, device_id_type=MESH)

        @pl.when(pos < count - 1)
        def _():
            pl.semaphore_signal(barrier, inc=1, device_id={axis: pos + 1}, device_id_type=MESH)

    for pos, count, low, high in ((me, ndepth, zlo, zhi), (mx, nimx, flo, fhi), (my, nimy, xlo, xhi)):
        @pl.when(pos == 0)
        def _():
            low[...] = jnp.zeros_like(low)

        @pl.when(pos == count - 1)
        def _():
            high[...] = jnp.zeros_like(high)

    peers = ndepth - 1
    for pos, count in ((mx, nimx), (my, nimy)):
        peers = peers + (pos + count - 1) // count + (2 * count - 2 - pos) // count
    pl.semaphore_wait(barrier, peers)
    loads[0].wait()

    def links(axis, pos, count, down_src, up_src, low, high, at):
        to_low = pltpu.make_async_remote_copy(
            src_ref=down_src, dst_ref=high, send_sem=halo_send.at[at], recv_sem=halo_recv.at[at],
            device_id={axis: lax.rem(pos + count - 1, count)}, device_id_type=MESH)
        to_high = pltpu.make_async_remote_copy(
            src_ref=up_src, dst_ref=low, send_sem=halo_send.at[at + 1], recv_sem=halo_recv.at[at + 1],
            device_id={axis: lax.rem(pos + 1, count)}, device_id_type=MESH)
        return pos, count, to_low, to_high

    def start(link):
        pos, count, to_low, to_high = link

        @pl.when(pos > 0)
        def _():
            to_low.start()

        @pl.when(pos < count - 1)
        def _():
            to_high.start()

    def finish(link):
        pos, count, to_low, to_high = link

        @pl.when(pos > 0)
        def _():
            to_low.wait_send()
            to_high.wait_recv()

        @pl.when(pos < count - 1)
        def _():
            to_high.wait_send()
            to_low.wait_recv()

    zlink = links("depth", me, ndepth, fb.at[0], fb.at[zdev - 1], zlo, zhi, 0)
    xlink = links("imy", my, nimy, fb.at[:, pl.ds(0, PACK)], fb.at[:, pl.ds(xdev - PACK, PACK)], xlo, xhi, 2)
    ylink = links("imx", mx, nimx, face, face, flo, fhi, 4)
    start(zlink)
    start(xlink)

    lane = iota((xdev, ydev), 1)

    def widen(z, packed):
        value = fb[z].astype(F32)
        vf[z + 1, SUB:SUB + xdev] = value
        return jnp.where(lane // 2 == z, pltpu.roll(value, 2 * z + 1, 1), packed)

    face[...] = lax.fori_loop(0, zdev, widen, jnp.zeros((xdev, ydev), F32), unroll=8).astype(BF16)
    start(ylink)

    for load in loads[1:]:
        load.wait()
    back = expand(order[...], xdev, ydev)
    factor = (2.0 * back - 1.0) * expand(live[0], xdev, ydev) * (step_len * LOG2E)
    flag[...] = back
    scales[...] = factor
    cen = [centers[j] for j in range(nb)]
    hei = [heights[j] for j in range(nb)]
    cur = []
    for j in range(nb):
        wid = jnp.full((rows_blk, ydev), widths[j], F32)
        cur.append((-0.5 * LOG2E) / (wid * wid))

    def absorb(i, carry):
        row = i * rows_blk
        here = pl.ds(pl.multiple_of(row, SUB), rows_blk)
        body = pl.ds(pl.multiple_of(row + SUB, SUB), rows_blk)
        fac = scales[here]

        def sample(z, carry):
            depth, gone = carry
            val = vf[z + 1, body]
            sigma = None
            for j in range(nb):
                off = val - cen[j]
                bump = jnp.exp2(off * cur[j] * off)
                lobes[j, z, here] = bump
                sigma = hei[j] * bump if sigma is None else sigma + hei[j] * bump
            depth = depth + sigma * fac
            now = jnp.exp2(depth)
            weights[z, here] = now - gone
            return depth, now

        zero = jnp.zeros((rows_blk, ydev), F32)
        depth, _ = lax.fori_loop(0, zdev, sample, (zero, zero + 1.0), unroll=8)
        mark = flag[here] > 0.5
        scales[here] = jnp.where(mark, jnp.exp2(-depth), -1.0)
        logs[here] = jnp.where(mark, -depth, depth) * (1.0 / LOG2E)
        return carry

    lax.fori_loop(0, xdev // rows_blk, absorb, 0)

    def log_copy(owner, source):
        return pltpu.make_async_remote_copy(
            src_ref=logs.at[pl.ds(pl.multiple_of(owner * rows_out, SUB), rows_out)], dst_ref=logs_in.at[source],
            send_sem=log_send.at[owner], recv_sem=log_recv.at[source], device_id={"depth": owner}, device_id_type=MESH)

    for step in range(1, ndepth):
        log_copy(lax.rem(me + step, ndepth), me).start()
    logs_in[me] = logs[pl.ds(pl.multiple_of(me * rows_out, SUB), rows_out)]
    finish(zlink)
    vf[0, SUB:SUB + xdev] = zlo[...].astype(F32)
    vf[zdev + 1, SUB:SUB + xdev] = zhi[...].astype(F32)
    finish(xlink)

    def widen_rows(z, carry):
        vf[z + 1, 0:SUB] = xlo[z].astype(F32)[PACK - SUB:]
        vf[z + 1, SUB + xdev:] = xhi[z].astype(F32)[:SUB]
        return carry

    lax.fori_loop(0, zdev, widen_rows, 0, unroll=4)
    finish(ylink)

    fromleft = pltpu.roll(flo[...].astype(F32), 1, 1)
    fromright = pltpu.roll(fhi[...].astype(F32), ydev - 1, 1)
    edges = jnp.where(lane % 2 == 0, fromright, fromleft)
    k_at, l_at = iota((2 * ydev, ydev), 0), iota((2 * ydev, ydev), 1)
    odd = k_at % 2 == 1
    plus = (k_at < ydev) & (k_at == l_at + 1) | (k_at >= ydev) & (l_at == ydev - 1) & jnp.logical_not(odd)
    minus = (k_at < ydev) & (k_at == l_at - 1) | (k_at >= ydev) & (l_at == 0) & odd
    slope = (plus.astype(F32) - minus.astype(F32)).astype(BF16)

    def across(z, carry):
        side = jnp.where(lane // 2 == z, edges, 0.0).astype(BF16)
        gy[z] = jnp.dot(jnp.concatenate([fb[z], side], axis=1), slope, preferred_element_type=F32)
        return carry

    lax.fori_loop(0, zdev, across, 0, unroll=16)

    def block(row):
        here = pl.ds(pl.multiple_of(row, SUB), rows_blk)
        body = pl.ds(pl.multiple_of(row + SUB, SUB), rows_blk)
        above = pl.ds(row + SUB - 1, rows_blk)
        below = pl.ds(row + SUB + 1, rows_blk)

        def sample(z, carry):
            prev, val, sums = carry
            after = vf[z + 2, body]
            dz = after - prev
            dx = vf[z + 1, below] - vf[z + 1, above]
            dy = gy[z, here]
            facing = (0.7 * 0.64) * dz + (0.7 * 0.48) * dx + (0.7 * 0.6) * dy
            shade = 0.3 + jnp.abs(facing) * lax.rsqrt(dz * dz + dx * dx + dy * dy + 4.0)
            weight = weights[z, here] * shade.astype(BF16).astype(F32)
            sums = tuple(acc + weight * lobes[j, z, here] for j, acc in enumerate(sums))
            return val, after, sums

        zero = jnp.zeros((rows_blk, ydev), F32)
        init = (vf[0, body], vf[1, body], (zero,) * nb)
        _, _, sums = lax.fori_loop(0, zdev, sample, init, unroll=8)
        scale = scales[here]
        chans = []
        for chan in range(3):
            total = None
            for j in range(nb):
                term = colours[j, chan] * sums[j]
                total = term if total is None else total + term
            chans.append(total * scale)
        return chans

    def tile(owner):
        def one(i, carry):
            local = pl.multiple_of(i * rows_blk, SUB)
            values = block(owner * rows_out + local)
            for chan, value in enumerate(values):
                stage[chan, pl.ds(local, rows_blk)] = value
            return carry

        lax.fori_loop(0, rows_out // rows_blk, one, 0)

    def sends(owner, source):
        place = {"depth": owner}
        return (
            pltpu.make_async_remote_copy(
                src_ref=tiles_out.at[owner], dst_ref=tiles_in.at[source], send_sem=tile_send.at[owner],
                recv_sem=tile_recv.at[source], device_id=place, device_id_type=MESH),
            pltpu.make_async_remote_copy(
                src_ref=peaks_out.at[owner], dst_ref=peaks_in.at[source], send_sem=peak_send.at[owner],
                recv_sem=peak_recv.at[source], device_id=place, device_id_type=MESH),
        )

    tiles_in[me] = jnp.zeros((3, rows_out, ydev), jnp.int16)
    peaks_in[me] = jnp.zeros((SUB, ydev), F32)

    def other(step, carry):
        owner = lax.rem(me + step, ndepth)
        tile(owner)
        line = iota((SUB, ydev), 0)
        peaks = jnp.zeros((SUB, ydev), F32)
        for chan in range(3):
            value = stage[chan]
            peak = jnp.maximum(jnp.max(value, axis=0, keepdims=True), 1e-30)
            peaks = jnp.where(line == chan, peak * (1.0 / LEVELS), peaks)
            tiles_out[owner, chan] = (value * (LEVELS / peak) + 0.5).astype(jnp.int32).astype(jnp.int16)
        peaks_out[owner] = peaks
        for copy in sends(owner, me):
            copy.start()
        return carry

    lax.fori_loop(1, ndepth, other, 0)
    tile(me)

    for step in range(1, ndepth):
        owner = lax.rem(me + step, ndepth)
        for copy in sends(owner, owner):
            copy.wait()
        log_copy(owner, owner).wait()

    mark = flag[pl.ds(pl.multiple_of(me * rows_out, SUB), rows_out)] > 0.5
    zero = jnp.zeros((rows_out, ydev), F32)
    done, through, total = [zero] * 3, zero + 1.0, zero
    for slab in range(ndepth):
        logt = logs_in[slab]
        clear = jnp.exp(logt)
        keep = jnp.where(mark, clear, 1.0)
        ahead = jnp.where(mark, 1.0, through)
        for chan in range(3):
            value = tiles_in[slab, chan].astype(jnp.int32).astype(F32) * peaks_in[slab, chan:chan + 1]
            value = jnp.where(me == slab, stage[chan], value)
            done[chan] = keep * done[chan] + ahead * value
        through = through * clear
        total = total + logt
    for chan in range(3):
        colour_out[chan] = done[chan]
    logt_out[...] = total


def local(field, brick_live, order, centers, widths, heights, colours):
    counts = tuple(lax.axis_size(axis) for axis in ("depth", "imx", "imy"))
    zdev, xdev, ydev = field.shape
    ndepth = counts[0]
    rows_out = xdev // ndepth
    step_len = OPTICAL / (zdev * ndepth)
    vmem = pl.BlockSpec(memory_space=pltpu.VMEM)
    dma = pltpu.SemaphoreType.DMA
    return pl.pallas_call(
        functools.partial(kernel, counts, step_len),
        out_shape=(
            pltpu.VMEM((3, rows_out, ydev), F32),
            pltpu.VMEM((rows_out, ydev), F32),
        ),
        in_specs=[pl.BlockSpec(memory_space=pl.ANY)] * 7,
        out_specs=(vmem, vmem),
        scratch_shapes=[
            pltpu.VMEM((zdev, xdev, ydev), BF16),
            pltpu.VMEM(brick_live.shape, jnp.int32),
            pltpu.VMEM(order.shape, jnp.int32),
            pltpu.SMEM(centers.shape, F32),
            pltpu.SMEM(widths.shape, F32),
            pltpu.SMEM(heights.shape, F32),
            pltpu.SMEM(colours.shape, F32),
            pltpu.VMEM((zdev + 2, xdev + 2 * SUB, ydev), F32),
            pltpu.VMEM((xdev, ydev), BF16),
            pltpu.VMEM((xdev, ydev), BF16),
            pltpu.VMEM((zdev, PACK, ydev), BF16),
            pltpu.VMEM((zdev, PACK, ydev), BF16),
            pltpu.VMEM((xdev, ydev), BF16),
            pltpu.VMEM((xdev, ydev), BF16),
            pltpu.VMEM((xdev, ydev), BF16),
            pltpu.VMEM((zdev, xdev, ydev), F32),
            pltpu.VMEM((centers.shape[0], zdev, xdev, ydev), F32),
            pltpu.VMEM((xdev, ydev), F32),
            pltpu.VMEM((xdev, ydev), F32),
            pltpu.VMEM((xdev, ydev), F32),
            pltpu.VMEM((ndepth, rows_out, ydev), F32),
            pltpu.VMEM((ndepth, 3, rows_out, ydev), jnp.int16),
            pltpu.VMEM((ndepth, 3, rows_out, ydev), jnp.int16),
            pltpu.VMEM((zdev, xdev, ydev), F32),
            pltpu.VMEM((3, rows_out, ydev), F32),
            pltpu.VMEM((ndepth, SUB, ydev), F32),
            pltpu.VMEM((ndepth, SUB, ydev), F32),
            dma((7,)),
            dma((6,)),
            dma((6,)),
            dma((ndepth,)),
            dma((ndepth,)),
            dma((ndepth,)),
            dma((ndepth,)),
            dma((ndepth,)),
            dma((ndepth,)),
        ],
        compiler_params=pltpu.CompilerParams(collective_id=0, has_side_effects=True),
    )(field, brick_live, order, centers, widths, heights, colours)


def solution(mesh):
    return jax.shard_map(
        local,
        mesh=mesh,
        in_specs=(
            P("depth", "imy", "imx"),
            P("depth", "imy", "imx"),
            P("imy", "imx"),
            P(),
            P(),
            P(),
            P(),
        ),
        out_specs=(P(None, ("imy", "depth"), "imx"), P(("imy", "depth"), "imx")),
        check_vma=False,
    )
```

profile of v0, /device:TPU:0, one launch (start us, length us, event | category | flops | bytes accessed | tf_op | source)
XLA Modules:
  0.0 16.6 jit_solution(17506402983406999276)
XLA Ops:
  0.6 14.7 %shard_map.86 = (f32[3,32,128]{2,1,0:T(8,128)S(1)}, f32[32,128]{1,0:T(8,128)S(1)}) custom-call(bf16[32,128,128]{2,1,0:T(8,128)(2,1)} %field.1, s32[1,4,4]{2,1,0:T(4,128)} %live_in.1, s32[16,16]{1,0:T(8,128)} %order_in.1, f32[4]{0:T(128)} %centers_in.1, f32[4]{0:T(128)} %widths_in.1, f32[4]{0:T(128)} %heights_in.1, f32[4,3]{1,0:T(4,128)} %colours_in.1), custom_call_target="tpu_custom_call" | custom-call | tf_op jit(solution)/shard_map/pallas_call | solution.py:317
  15.4 0.6 %copy.11 = f32[3,32,128]{2,1,0:T(8,128)} copy(f32[3,32,128]{2,1,0:T(8,128)S(1)} %get-tuple-element.2) | data formatting | bytes 98304
  16.0 0.6 %copy.12 = f32[32,128]{1,0:T(8,128)} copy(f32[32,128]{1,0:T(8,128)S(1)} %get-tuple-element.3) | data formatting | bytes 32768
where the time goes:
time: 16.8 us; the launch traced here: 16.6 us
  Pallas kernels  14.7 us (88%)
  local copies, waits for them, and re-layouts  1.23 us (7%)
  between operations  0.64 us (4%)
    pallas_call x1, Pallas kernels, local(): pl.pallas_call(functools.partial(kernel, counts, step_len), out_shape=(pl...  14.7 us
    unnamed x2, local copies, waits for them, and re-layouts  1.23 us

commit v1 on v0

v1 whole, which is shorter than its diff:
```python
import functools
import math

import jax
import jax.numpy as jnp
from jax import lax
from jax.experimental import pallas as pl
from jax.experimental.pallas import tpu as pltpu
from jax.sharding import PartitionSpec as P

OPTICAL = 3.0
MESH = pl.DeviceIdType.MESH
SUB = 8
PACK = 16
F32 = jnp.float32
BF16 = jnp.bfloat16
LEVELS = 32000.0
UNROLL_A = 16
CHUNK = 16
PIECES = 4
LOG2E = math.log2(math.e)


def iota(shape, dim):
    return lax.broadcasted_iota(jnp.int32, shape, dim)


def expand(small, rows, cols):
    high, wide = small.shape
    down = (iota((rows, high), 0) // (rows // high) == iota((rows, high), 1)).astype(F32).astype(BF16)
    along = (iota((wide, cols), 1) // (cols // wide) == iota((wide, cols), 0)).astype(F32).astype(BF16)
    tall = jnp.dot(down, small.astype(F32).astype(BF16), preferred_element_type=F32)
    return jnp.dot(tall.astype(BF16), along, preferred_element_type=F32)


def kernel(
    counts, step_len,
    field, live_in, order_in, centers_in, widths_in, heights_in, colours_in,
    colour_out, logt_out,
    fb, live, order, centers, widths, heights, colours,
    vf, zlo, zhi, xlo, xhi, face, flo, fhi, edges, slopes, weights, lobes, scales, flag, logs, logs_in,
    tiles_out, tiles_in, stage, own, peaks_out, peaks_in,
    load_sem, piece_sem, halo_send, halo_recv, log_send, log_recv, tile_send, tile_recv, peak_send, peak_recv,
):
    ndepth, nimx, nimy = counts
    me = lax.axis_index("depth")
    mx = lax.axis_index("imx")
    my = lax.axis_index("imy")
    zdev, xdev, ydev = fb.shape
    rows_out = xdev // ndepth
    nb = centers.shape[0]
    unit = max(PACK, rows_out)
    units, per_unit, owners = xdev // unit, unit // PACK, unit // rows_out
    blocks = units * per_unit
    span = zdev // PIECES

    def at_turn(turn):
        if owners > 1:
            return turn
        return jnp.where(turn < me, turn, ndepth - 1 - turn + me)

    def rows_of(place):
        return pl.ds(pl.multiple_of(place * unit, PACK), unit)

    def piece_load(piece):
        part = pl.ds(piece * span, span)
        return pltpu.make_async_copy(field.at[part], fb.at[part], piece_sem.at[piece])

    for piece in range(PIECES):
        piece_load(piece).start()
    pairs = ((order_in, order), (live_in, live), (centers_in, centers),
             (widths_in, widths), (heights_in, heights), (colours_in, colours))
    loads = [pltpu.make_async_copy(src, dst, load_sem.at[at]) for at, (src, dst) in enumerate(pairs)]
    for load in loads:
        load.start()

    barrier = pltpu.get_barrier_semaphore()
    for step in range(1, ndepth):
        pl.semaphore_signal(barrier, inc=1, device_id={"depth": lax.rem(me + step, ndepth)}, device_id_type=MESH)
    for axis, pos, count in (("imx", mx, nimx), ("imy", my, nimy)):
        @pl.when(pos > 0)
        def _():
            pl.semaphore_signal(barrier, inc=1, device_id={axis: pos - 1}, device_id_type=MESH)

        @pl.when(pos < count - 1)
        def _():
            pl.semaphore_signal(barrier, inc=1, device_id={axis: pos + 1}, device_id_type=MESH)

    for pos, count, low, high in ((me, ndepth, zlo, zhi), (mx, nimx, flo, fhi), (my, nimy, xlo, xhi)):
        @pl.when(pos == 0)
        def _():
            low[...] = jnp.zeros(low.shape, BF16)

        @pl.when(pos == count - 1)
        def _():
            high[...] = jnp.zeros(high.shape, BF16)

    def links(axis, pos, count, down_src, up_src, low, high, at):
        to_low = pltpu.make_async_remote_copy(
            src_ref=down_src, dst_ref=high, send_sem=halo_send.at[at], recv_sem=halo_recv.at[at],
            device_id={axis: lax.rem(pos + count - 1, count)}, device_id_type=MESH)
        to_high = pltpu.make_async_remote_copy(
            src_ref=up_src, dst_ref=low, send_sem=halo_send.at[at + 1], recv_sem=halo_recv.at[at + 1],
            device_id={axis: lax.rem(pos + 1, count)}, device_id_type=MESH)
        return pos, count, to_low, to_high

    def start(link):
        pos, count, to_low, to_high = link

        @pl.when(pos > 0)
        def _():
            to_low.start()

        @pl.when(pos < count - 1)
        def _():
            to_high.start()

    def finish(link):
        pos, count, to_low, to_high = link

        @pl.when(pos > 0)
        def _():
            to_low.wait_send()
            to_high.wait_recv()

        @pl.when(pos < count - 1)
        def _():
            to_high.wait_send()
            to_low.wait_recv()

    def zlink():
        return links("depth", me, ndepth, field.at[0], field.at[zdev - 1], zlo, zhi, 0)

    def ylink():
        return links("imx", mx, nimx, face, face, flo, fhi, 2)

    def xlink():
        return links("imy", my, nimy, field.at[:, pl.ds(0, PACK)], field.at[:, pl.ds(xdev - PACK, PACK)], xlo, xhi, 4)

    for load in loads:
        load.wait()
    back = expand(order[...], xdev, ydev)
    factor = (2.0 * back - 1.0) * expand(live[0], xdev, ydev) * (step_len * LOG2E)
    flag[...] = back
    scales[...] = factor
    cen = [centers[j] for j in range(nb)]
    hei = [heights[j] for j in range(nb)]
    cur = []
    for j in range(nb):
        wid = jnp.full((PACK, ydev), widths[j], F32)
        cur.append((-0.5 * LOG2E) / (wid * wid))
    lane = iota((PACK, ydev), 1)

    def absorb(row):
        here = pl.ds(pl.multiple_of(row, PACK), PACK)
        body = pl.ds(pl.multiple_of(row + SUB, SUB), PACK)
        fac = scales[here]
        amount = [hei[j] * fac for j in range(nb)]

        def sample(z, carry):
            depth, gone = carry
            val = fb[z, here].astype(F32)
            vf[z + 1, body] = val
            terms = []
            for j in range(nb):
                off = val - cen[j]
                if j == 0:
                    slopes[z, here] = pltpu.roll(off, ydev - 1, 1) - pltpu.roll(off, 1, 1)
                bump = jnp.exp2(off * cur[j] * off)
                lobes[j, z, here] = bump
                terms.append(amount[j] * bump)
            while len(terms) > 1:
                terms = [sum(terms[at:at + 2][1:], terms[at]) for at in range(0, len(terms), 2)]
            depth = depth + terms[0]
            now = jnp.exp2(depth)
            weights[z, here] = now - gone
            return depth, now

        zero = jnp.zeros((PACK, ydev), F32)
        depth, _ = lax.fori_loop(0, zdev, sample, (zero, zero + 1.0), unroll=UNROLL_A)
        mark = flag[here] > 0.5
        scales[here] = jnp.where(mark, jnp.exp2(-depth), -1.0)
        logs[here] = jnp.where(mark, -depth, depth) * (1.0 / LOG2E)

    def log_copy(owner, source):
        return pltpu.make_async_remote_copy(
            src_ref=logs.at[pl.ds(pl.multiple_of(owner * rows_out, SUB), rows_out)], dst_ref=logs_in.at[source],
            send_sem=log_send.at[owner], recv_sem=log_recv.at[source], device_id={"depth": owner}, device_id_type=MESH)

    def send_logs(turn, carry):
        for sub in range(owners):
            owner = at_turn(turn) * owners + sub

            @pl.when(owner != me)
            def _():
                log_copy(owner, me).start()

        return carry

    def absorb_turn(turn, carry):
        place = at_turn(turn)

        def one(i, inside):
            absorb(place * unit + i * PACK)
            return inside

        return lax.fori_loop(0, per_unit, one, carry)

    wide = iota((xdev, ydev), 1) // 2
    packed = jnp.zeros((xdev, ydev), BF16)
    for piece in range(PIECES):
        piece_load(piece).wait()
        for z in range(piece * span, piece * span + span):
            packed = jnp.where(wide == z, pltpu.roll(fb[z], 2 * z + 1, 1), packed)
    face[...] = packed

    peers = ndepth - 1
    for pos, count in ((mx, nimx), (my, nimy)):
        peers = peers + (pos + count - 1) // count + (2 * count - 2 - pos) // count
    pl.semaphore_wait(barrier, peers)
    start(ylink())
    start(zlink())
    start(xlink())

    def next_turn(turn, carry):
        absorb_turn(turn, carry)
        return send_logs(turn, carry)

    lax.fori_loop(0, units, next_turn, 0)

    outermost = (lane == 0) | (lane == ydev - 1)

    def row_of(at):
        return at_turn(at // per_unit) * unit + at % per_unit * PACK

    def patch(first, count, row):
        here = pl.ds(pl.multiple_of(row, PACK), PACK)
        outer = edges[here]
        for z in range(count):
            edge = pltpu.roll(outer, ydev - 1 - 2 * (first + z), 1)
            pltpu.store(slopes.at[first + z, here], slopes[first + z, here] + edge, mask=outermost)

    def block(at):
        row = row_of(at)
        following = row_of(jnp.minimum(at + 1, blocks - 1))
        here = pl.ds(pl.multiple_of(row, PACK), PACK)
        body = pl.ds(pl.multiple_of(row + SUB, SUB), PACK)
        above = pl.ds(row + SUB - 1, PACK)
        below = pl.ds(row + SUB + 1, PACK)

        def chunk(c, carry):
            prev, val, sums = carry
            for i in range(CHUNK):
                z = c * CHUNK + i
                after = vf[z + 2, body]
                dz = after - prev
                dx = vf[z + 1, below] - vf[z + 1, above]
                dy = slopes[z, here]
                facing = (0.7 * 0.64) * dz + (0.7 * 0.48) * dx + (0.7 * 0.6) * dy
                shade = 0.3 + jnp.abs(facing) * lax.rsqrt(dz * dz + dx * dx + dy * dy + 4.0)
                weight = weights[z, here] * shade.astype(BF16).astype(F32)
                sums = tuple(acc + weight * lobes[j, z, here] for j, acc in enumerate(sums))
                prev, val = val, after
            patch(c * CHUNK, CHUNK, following)
            return prev, val, sums

        zero = jnp.zeros((PACK, ydev), F32)
        init = (vf[0, body], vf[1, body], (zero,) * nb)
        _, _, sums = lax.fori_loop(0, zdev // CHUNK, chunk, init)
        scale = scales[here]
        spot = pl.ds(pl.multiple_of(at % per_unit * PACK, PACK), PACK)
        for chan in range(3):
            total = None
            for j in range(nb):
                term = colours[j, chan] * sums[j]
                total = term if total is None else total + term
            stage[chan, spot] = total * scale

    def sends(owner, source):
        place = {"depth": owner}
        return (
            pltpu.make_async_remote_copy(
                src_ref=tiles_out.at[owner], dst_ref=tiles_in.at[source], send_sem=tile_send.at[owner],
                recv_sem=tile_recv.at[source], device_id=place, device_id_type=MESH),
            pltpu.make_async_remote_copy(
                src_ref=peaks_out.at[owner], dst_ref=peaks_in.at[source], send_sem=peak_send.at[owner],
                recv_sem=peak_recv.at[source], device_id=place, device_id_type=MESH),
        )

    tiles_in[me] = jnp.zeros((3, rows_out, ydev), jnp.int16)
    peaks_in[me] = jnp.zeros((SUB, ydev), F32)
    finish(xlink())

    def widen_rows(z, carry):
        vf[z + 1, 0:SUB] = xlo[z].astype(F32)[PACK - SUB:]
        vf[z + 1, SUB + xdev:] = xhi[z].astype(F32)[:SUB]
        return carry

    lax.fori_loop(0, zdev, widen_rows, 0, unroll=8)
    finish(zlink())
    vf[0, SUB:SUB + xdev] = zlo[...].astype(F32)
    vf[zdev + 1, SUB:SUB + xdev] = zhi[...].astype(F32)
    finish(ylink())
    mine = face[...].astype(F32)
    low = pltpu.roll(mine - flo[...].astype(F32), 1, 1)
    high = pltpu.roll(fhi[...].astype(F32) - mine, ydev - 1, 1)
    edges[...] = jnp.where(iota((xdev, ydev), 1) % 2 == 0, high, low)
    patch(0, zdev, row_of(0))

    def tile_turn(turn):
        place = at_turn(turn)
        for sub in range(owners):
            owner = place * owners + sub
            part = pl.ds(sub * rows_out, rows_out)

            @pl.when(owner == me)
            def _():
                own[...] = stage[:, part]

            @pl.when(owner != me)
            def _():
                line = iota((SUB, ydev), 0)
                peaks = jnp.zeros((SUB, ydev), F32)
                for chan in range(3):
                    value = stage[chan, part]
                    peak = jnp.maximum(jnp.max(value, axis=0, keepdims=True), 1e-30)
                    peaks = jnp.where(line == chan, peak * (1.0 / LEVELS), peaks)
                    tiles_out[owner, chan] = (value * (LEVELS / peak) + 0.5).astype(jnp.int32).astype(jnp.int16)
                peaks_out[owner] = peaks
                for copy in sends(owner, me):
                    copy.start()

    def step(at, carry):
        turn = at // per_unit
        final = at % per_unit == per_unit - 1

        block(at)

        @pl.when(final)
        def _():
            tile_turn(turn)

        return carry

    lax.fori_loop(0, blocks, step, 0)

    for step_on in range(1, ndepth):
        owner = lax.rem(me + step_on, ndepth)
        for copy in sends(owner, owner):
            copy.wait()
        log_copy(owner, owner).wait()

    logs_in[me] = logs[pl.ds(pl.multiple_of(me * rows_out, SUB), rows_out)]
    mark = flag[pl.ds(pl.multiple_of(me * rows_out, SUB), rows_out)] > 0.5
    zero = jnp.zeros((rows_out, ydev), F32)
    done, through, total = [zero] * 3, zero + 1.0, zero
    for slab in range(ndepth):
        logt = logs_in[slab]
        clear = jnp.exp(logt)
        keep = jnp.where(mark, clear, 1.0)
        ahead = jnp.where(mark, 1.0, through)
        for chan in range(3):
            value = tiles_in[slab, chan].astype(jnp.int32).astype(F32) * peaks_in[slab, chan:chan + 1]
            value = jnp.where(me == slab, own[chan], value)
            done[chan] = keep * done[chan] + ahead * value
        through = through * clear
        total = total + logt
    for chan in range(3):
        colour_out[chan] = done[chan]
    logt_out[...] = total


def local(field, brick_live, order, centers, widths, heights, colours):
    counts = tuple(lax.axis_size(axis) for axis in ("depth", "imx", "imy"))
    zdev, xdev, ydev = field.shape
    ndepth = counts[0]
    rows_out = xdev // ndepth
    step_len = OPTICAL / (zdev * ndepth)
    unit = max(PACK, rows_out)
    units = xdev // unit
    vmem = pl.BlockSpec(memory_space=pltpu.VMEM)
    dma = pltpu.SemaphoreType.DMA
    return pl.pallas_call(
        functools.partial(kernel, counts, step_len),
        out_shape=(
            pltpu.VMEM((3, rows_out, ydev), F32),
            pltpu.VMEM((rows_out, ydev), F32),
        ),
        in_specs=[pl.BlockSpec(memory_space=pl.ANY)] * 7,
        out_specs=(vmem, vmem),
        scratch_shapes=[
            pltpu.VMEM((zdev, xdev, ydev), BF16),
            pltpu.VMEM(brick_live.shape, jnp.int32),
            pltpu.VMEM(order.shape, jnp.int32),
            pltpu.SMEM(centers.shape, F32),
            pltpu.SMEM(widths.shape, F32),
            pltpu.SMEM(heights.shape, F32),
            pltpu.SMEM(colours.shape, F32),
            pltpu.VMEM((zdev + 2, xdev + 2 * SUB, ydev), F32),
            pltpu.VMEM((xdev, ydev), BF16),
            pltpu.VMEM((xdev, ydev), BF16),
            pltpu.VMEM((zdev, PACK, ydev), BF16),
            pltpu.VMEM((zdev, PACK, ydev), BF16),
            pltpu.VMEM((xdev, ydev), BF16),
            pltpu.VMEM((xdev, ydev), BF16),
            pltpu.VMEM((xdev, ydev), BF16),
            pltpu.VMEM((xdev, ydev), F32),
            pltpu.VMEM((zdev, xdev, ydev), F32),
            pltpu.VMEM((zdev, xdev, ydev), F32),
            pltpu.VMEM((centers.shape[0], zdev, xdev, ydev), F32),
            pltpu.VMEM((xdev, ydev), F32),
            pltpu.VMEM((xdev, ydev), F32),
            pltpu.VMEM((xdev, ydev), F32),
            pltpu.VMEM((ndepth, rows_out, ydev), F32),
            pltpu.VMEM((ndepth, 3, rows_out, ydev), jnp.int16),
            pltpu.VMEM((ndepth, 3, rows_out, ydev), jnp.int16),
            pltpu.VMEM((3, unit, ydev), F32),
            pltpu.VMEM((3, rows_out, ydev), F32),
            pltpu.VMEM((ndepth, SUB, ydev), F32),
            pltpu.VMEM((ndepth, SUB, ydev), F32),
            dma((6,)),
            dma((PIECES,)),
            dma((6,)),
            dma((6,)),
            dma((ndepth,)),
            dma((ndepth,)),
            dma((ndepth,)),
            dma((ndepth,)),
            dma((ndepth,)),
            dma((ndepth,)),
        ],
        compiler_params=pltpu.CompilerParams(collective_id=0, has_side_effects=True),
    )(field, brick_live, order, centers, widths, heights, colours)


def solution(mesh):
    return jax.shard_map(
        local,
        mesh=mesh,
        in_specs=(
            P("depth", "imy", "imx"),
            P("depth", "imy", "imx"),
            P("imy", "imx"),
            P(),
            P(),
            P(),
            P(),
        ),
        out_specs=(P(None, ("imy", "depth"), "imx"), P(("imy", "depth"), "imx")),
        check_vma=False,
    )
```

time: 16.8 us -> 15.5 us (0.923)
  Pallas kernels: 14.7 us -> 13.4 us
    pallas_call x1, Pallas kernels: 14.7 us -> 13.4 us  [local(): pl.pallas_call(functools.partial(kernel, counts, step_len), out_shape=(pl...]
where the time goes in v1:
time: 15.5 us; the launch traced here: 15.2 us
  Pallas kernels  13.4 us (86%)
  local copies, waits for them, and re-layouts  1.23 us (8%)
  between operations  0.64 us (4%)
    pallas_call x1, Pallas kernels, local(): pl.pallas_call(functools.partial(kernel, counts, step_len), out_shape=(pl...  13.4 us
    unnamed x2, local copies, waits for them, and re-layouts  1.23 us

profile of v1, /device:TPU:0, one launch (start us, length us, event | category | flops | bytes accessed | tf_op | source)
XLA Modules:
  0.0 15.2 jit_solution(13028544134368174910)
XLA Ops:
  0.6 13.4 %shard_map.86 = (f32[3,32,128]{2,1,0:T(8,128)S(1)}, f32[32,128]{1,0:T(8,128)S(1)}) custom-call(bf16[32,128,128]{2,1,0:T(8,128)(2,1)} %field.1, s32[1,4,4]{2,1,0:T(4,128)} %live_in.1, s32[16,16]{1,0:T(8,128)} %order_in.1, f32[4]{0:T(128)} %centers_in.1, f32[4]{0:T(128)} %widths_in.1, f32[4]{0:T(128)} %heights_in.1, f32[4,3]{1,0:T(4,128)} %colours_in.1), custom_call_target="tpu_custom_call" | custom-call | tf_op jit(solution)/shard_map/pallas_call | solution.py:383
  14.0 0.6 %copy.11 = f32[3,32,128]{2,1,0:T(8,128)} copy(f32[3,32,128]{2,1,0:T(8,128)S(1)} %get-tuple-element.2) | data formatting | bytes 98304
  14.6 0.6 %copy.12 = f32[32,128]{1,0:T(8,128)} copy(f32[32,128]{1,0:T(8,128)S(1)} %get-tuple-element.3) | data formatting | bytes 32768

commit v2 on v1

--- a/solution.py
+++ b/solution.py
@@ -18,6 +18,7 @@
 UNROLL_A = 16
 CHUNK = 16
 PIECES = 4
+EARLY = 0
 LOG2E = math.log2(math.e)
 
 
@@ -38,9 +39,9 @@
     field, live_in, order_in, centers_in, widths_in, heights_in, colours_in,
     colour_out, logt_out,
     fb, live, order, centers, widths, heights, colours,
-    vf, zlo, zhi, xlo, xhi, face, flo, fhi, edges, slopes, weights, lobes, scales, flag, logs, logs_in,
-    tiles_out, tiles_in, stage, own, peaks_out, peaks_in,
-    load_sem, piece_sem, halo_send, halo_recv, log_send, log_recv, tile_send, tile_recv, peak_send, peak_recv,
+    vf, zlo, zhi, xlo, xhi, face, flo, fhi, edges, slopes, splats, weights, lobes, scales, flag, logs, logs_in,
+    tiles_out, tiles_in, stage, own,
+    load_sem, piece_sem, halo_send, halo_recv, log_send, log_recv, tile_send, tile_recv,
 ):
     ndepth, nimx, nimy = counts
     me = lax.axis_index("depth")
@@ -53,6 +54,8 @@
     units, per_unit, owners = xdev // unit, unit // PACK, unit // rows_out
     blocks = units * per_unit
     span = zdev // PIECES
+    early = jnp.clip(ndepth - 1 - 2 * me, 0, min(EARLY, units))
+    plane = max(PACK, rows_out)
 
     def at_turn(turn):
         if owners > 1:
@@ -66,25 +69,26 @@
         part = pl.ds(piece * span, span)
         return pltpu.make_async_copy(field.at[part], fb.at[part], piece_sem.at[piece])
 
-    for piece in range(PIECES):
-        piece_load(piece).start()
+    barrier = pltpu.get_barrier_semaphore()
+    for axis, pos, count in (("imx", mx, nimx), ("imy", my, nimy)):
+        @pl.when(pos > 0)
+        def _():
+            pl.semaphore_signal(barrier, inc=1, device_id={axis: pos - 1}, device_id_type=MESH)
+
+        @pl.when(pos < count - 1)
+        def _():
+            pl.semaphore_signal(barrier, inc=1, device_id={axis: pos + 1}, device_id_type=MESH)
+
+    for step in range(1, ndepth):
+        pl.semaphore_signal(barrier, inc=1, device_id={"depth": lax.rem(me + step, ndepth)}, device_id_type=MESH)
+
     pairs = ((order_in, order), (live_in, live), (centers_in, centers),
              (widths_in, widths), (heights_in, heights), (colours_in, colours))
     loads = [pltpu.make_async_copy(src, dst, load_sem.at[at]) for at, (src, dst) in enumerate(pairs)]
     for load in loads:
         load.start()
-
-    barrier = pltpu.get_barrier_semaphore()
-    for step in range(1, ndepth):
-        pl.semaphore_signal(barrier, inc=1, device_id={"depth": lax.rem(me + step, ndepth)}, device_id_type=MESH)
-    for axis, pos, count in (("imx", mx, nimx), ("imy", my, nimy)):
-        @pl.when(pos > 0)
-        def _():
-            pl.semaphore_signal(barrier, inc=1, device_id={axis: pos - 1}, device_id_type=MESH)
-
-        @pl.when(pos < count - 1)
-        def _():
-            pl.semaphore_signal(barrier, inc=1, device_id={axis: pos + 1}, device_id_type=MESH)
+    for piece in range(PIECES):
+        piece_load(piece).start()
 
     for pos, count, low, high in ((me, ndepth, zlo, zhi), (mx, nimx, flo, fhi), (my, nimy, xlo, xhi)):
         @pl.when(pos == 0)
@@ -128,14 +132,16 @@
             to_high.wait_send()
             to_low.wait_recv()
 
-    def zlink():
-        return links("depth", me, ndepth, field.at[0], field.at[zdev - 1], zlo, zhi, 0)
-
-    def ylink():
-        return links("imx", mx, nimx, face, face, flo, fhi, 2)
+    def zlink(place):
+        rows = rows_of(place)
+        return links("depth", me, ndepth, field.at[0, rows], field.at[zdev - 1, rows], zlo.at[rows], zhi.at[rows], 2 * place)
+
+    def ylink(place):
+        rows = rows_of(place)
+        return links("imx", mx, nimx, face.at[rows], face.at[rows], flo.at[rows], fhi.at[rows], 2 * units + 2 * place)
 
     def xlink():
-        return links("imy", my, nimy, field.at[:, pl.ds(0, PACK)], field.at[:, pl.ds(xdev - PACK, PACK)], xlo, xhi, 4)
+        return links("imy", my, nimy, field.at[:, pl.ds(0, PACK)], field.at[:, pl.ds(xdev - PACK, PACK)], xlo, xhi, 4 * units)
 
     for load in loads:
         load.wait()
@@ -143,19 +149,18 @@
     factor = (2.0 * back - 1.0) * expand(live[0], xdev, ydev) * (step_len * LOG2E)
     flag[...] = back
     scales[...] = factor
-    cen = [centers[j] for j in range(nb)]
-    hei = [heights[j] for j in range(nb)]
-    cur = []
     for j in range(nb):
         wid = jnp.full((PACK, ydev), widths[j], F32)
-        cur.append((-0.5 * LOG2E) / (wid * wid))
+        splats[0, j] = jnp.full((PACK, ydev), centers[j], F32)
+        splats[1, j] = (-0.5 * LOG2E) / (wid * wid)
     lane = iota((PACK, ydev), 1)
 
     def absorb(row):
         here = pl.ds(pl.multiple_of(row, PACK), PACK)
         body = pl.ds(pl.multiple_of(row + SUB, SUB), PACK)
         fac = scales[here]
-        amount = [hei[j] * fac for j in range(nb)]
+        for j in range(nb):
+            splats[2, j] = heights[j] * fac
 
         def sample(z, carry):
             depth, gone = carry
@@ -163,12 +168,12 @@
             vf[z + 1, body] = val
             terms = []
             for j in range(nb):
-                off = val - cen[j]
+                off = val - splats[0, j]
                 if j == 0:
                     slopes[z, here] = pltpu.roll(off, ydev - 1, 1) - pltpu.roll(off, 1, 1)
-                bump = jnp.exp2(off * cur[j] * off)
+                bump = jnp.exp2(off * splats[1, j] * off)
                 lobes[j, z, here] = bump
-                terms.append(amount[j] * bump)
+                terms.append(splats[2, j] * bump)
             while len(terms) > 1:
                 terms = [sum(terms[at:at + 2][1:], terms[at]) for at in range(0, len(terms), 2)]
             depth = depth + terms[0]
@@ -214,19 +219,29 @@
             packed = jnp.where(wide == z, pltpu.roll(fb[z], 2 * z + 1, 1), packed)
     face[...] = packed
 
+    if EARLY:
+        lax.fori_loop(0, early, absorb_turn, 0)
     peers = ndepth - 1
     for pos, count in ((mx, nimx), (my, nimy)):
         peers = peers + (pos + count - 1) // count + (2 * count - 2 - pos) // count
     pl.semaphore_wait(barrier, peers)
-    start(ylink())
-    start(zlink())
+
+    def start_turn(turn, carry):
+        start(ylink(at_turn(turn)))
+        start(zlink(at_turn(turn)))
+        return carry
+
+    start_turn(0, 0)
     start(xlink())
+    lax.fori_loop(1, units, start_turn, 0)
+    if EARLY:
+        lax.fori_loop(0, early, send_logs, 0)
 
     def next_turn(turn, carry):
         absorb_turn(turn, carry)
         return send_logs(turn, carry)
 
-    lax.fori_loop(0, units, next_turn, 0)
+    lax.fori_loop(early if EARLY else 0, units, next_turn, 0)
 
     outermost = (lane == 0) | (lane == ydev - 1)
 
@@ -276,19 +291,12 @@
                 total = term if total is None else total + term
             stage[chan, spot] = total * scale
 
-    def sends(owner, source):
-        place = {"depth": owner}
-        return (
-            pltpu.make_async_remote_copy(
-                src_ref=tiles_out.at[owner], dst_ref=tiles_in.at[source], send_sem=tile_send.at[owner],
-                recv_sem=tile_recv.at[source], device_id=place, device_id_type=MESH),
-            pltpu.make_async_remote_copy(
-                src_ref=peaks_out.at[owner], dst_ref=peaks_in.at[source], send_sem=peak_send.at[owner],
-                recv_sem=peak_recv.at[source], device_id=place, device_id_type=MESH),
-        )
-
-    tiles_in[me] = jnp.zeros((3, rows_out, ydev), jnp.int16)
-    peaks_in[me] = jnp.zeros((SUB, ydev), F32)
+    def tile_copy(owner, source):
+        return pltpu.make_async_remote_copy(
+            src_ref=tiles_out.at[owner], dst_ref=tiles_in.at[source], send_sem=tile_send.at[owner],
+            recv_sem=tile_recv.at[source], device_id={"depth": owner}, device_id_type=MESH)
+
+    tiles_in[me] = jnp.zeros(tiles_in.shape[1:], jnp.int16)
     finish(xlink())
 
     def widen_rows(z, carry):
@@ -297,14 +305,20 @@
         return carry
 
     lax.fori_loop(0, zdev, widen_rows, 0, unroll=8)
-    finish(zlink())
-    vf[0, SUB:SUB + xdev] = zlo[...].astype(F32)
-    vf[zdev + 1, SUB:SUB + xdev] = zhi[...].astype(F32)
-    finish(ylink())
-    mine = face[...].astype(F32)
-    low = pltpu.roll(mine - flo[...].astype(F32), 1, 1)
-    high = pltpu.roll(fhi[...].astype(F32) - mine, ydev - 1, 1)
-    edges[...] = jnp.where(iota((xdev, ydev), 1) % 2 == 0, high, low)
+    def ready(turn):
+        place = at_turn(turn)
+        rows = rows_of(place)
+        body = pl.ds(pl.multiple_of(place * unit + SUB, SUB), unit)
+        finish(zlink(place))
+        vf[0, body] = zlo[rows].astype(F32)
+        vf[zdev + 1, body] = zhi[rows].astype(F32)
+        finish(ylink(place))
+        mine = face[rows].astype(F32)
+        low = pltpu.roll(mine - flo[rows].astype(F32), 1, 1)
+        high = pltpu.roll(fhi[rows].astype(F32) - mine, ydev - 1, 1)
+        edges[rows] = jnp.where(iota((unit, ydev), 1) % 2 == 0, high, low)
+
+    ready(0)
     patch(0, zdev, row_of(0))
 
     def tile_turn(turn):
@@ -319,21 +333,26 @@
 
             @pl.when(owner != me)
             def _():
-                line = iota((SUB, ydev), 0)
-                peaks = jnp.zeros((SUB, ydev), F32)
+                line = iota((PACK, ydev), 0)
+                powers = jnp.zeros((PACK, ydev), F32)
                 for chan in range(3):
                     value = stage[chan, part]
                     peak = jnp.maximum(jnp.max(value, axis=0, keepdims=True), 1e-30)
-                    peaks = jnp.where(line == chan, peak * (1.0 / LEVELS), peaks)
-                    tiles_out[owner, chan] = (value * (LEVELS / peak) + 0.5).astype(jnp.int32).astype(jnp.int16)
-                peaks_out[owner] = peaks
-                for copy in sends(owner, me):
-                    copy.start()
+                    power = jnp.ceil(jnp.log2(peak * (1.0 / LEVELS)))
+                    powers = jnp.where(line == chan, power, powers)
+                    level = (value * jnp.exp2(-power) + 0.5).astype(jnp.int32)
+                    tiles_out[owner, chan * plane:chan * plane + rows_out] = level.astype(jnp.int16)
+                tiles_out[owner, 3 * plane:] = powers.astype(jnp.int32).astype(jnp.int16)
+                tile_copy(owner, me).start()
 
     def step(at, carry):
         turn = at // per_unit
         final = at % per_unit == per_unit - 1
 
+        @pl.when(final & (turn < units - 1))
+        def _():
+            ready(turn + 1)
+
         block(at)
 
         @pl.when(final)
@@ -343,31 +362,40 @@
         return carry
 
     lax.fori_loop(0, blocks, step, 0)
-
-    for step_on in range(1, ndepth):
-        owner = lax.rem(me + step_on, ndepth)
-        for copy in sends(owner, owner):
-            copy.wait()
-        log_copy(owner, owner).wait()
 
     logs_in[me] = logs[pl.ds(pl.multiple_of(me * rows_out, SUB), rows_out)]
     mark = flag[pl.ds(pl.multiple_of(me * rows_out, SUB), rows_out)] > 0.5
     zero = jnp.zeros((rows_out, ydev), F32)
     done, through, total = [zero] * 3, zero + 1.0, zero
     for slab in range(ndepth):
+        @pl.when(me != slab)
+        def _():
+            log_copy(slab, slab).wait()
+            tile_copy(slab, slab).wait()
+
         logt = logs_in[slab]
         clear = jnp.exp(logt)
         keep = jnp.where(mark, clear, 1.0)
         ahead = jnp.where(mark, 1.0, through)
+        powers = jnp.exp2(tiles_in[slab, 3 * plane:].astype(jnp.int32).astype(F32))
         for chan in range(3):
-            value = tiles_in[slab, chan].astype(jnp.int32).astype(F32) * peaks_in[slab, chan:chan + 1]
-            value = jnp.where(me == slab, own[chan], value)
+            level = tiles_in[slab, chan * plane:chan * plane + rows_out].astype(jnp.int32).astype(F32)
+            value = jnp.where(me == slab, own[chan], level * powers[chan:chan + 1])
             done[chan] = keep * done[chan] + ahead * value
         through = through * clear
         total = total + logt
     for chan in range(3):
         colour_out[chan] = done[chan]
     logt_out[...] = total
+
+
+def hand_over(colour, logt, colour_out, logt_out, sem):
+    copies = [pltpu.make_async_copy(src, dst, sem.at[at])
+              for at, (src, dst) in enumerate(((colour, colour_out), (logt, logt_out)))]
+    for copy in copies:
+        copy.start()
+    for copy in copies:
+        copy.wait()
 
 
 def local(field, brick_live, order, centers, widths, heights, colours):
@@ -380,7 +408,7 @@
     units = xdev // unit
     vmem = pl.BlockSpec(memory_space=pltpu.VMEM)
     dma = pltpu.SemaphoreType.DMA
-    return pl.pallas_call(
+    done = pl.pallas_call(
         functools.partial(kernel, counts, step_len),
         out_shape=(
             pltpu.VMEM((3, rows_out, ydev), F32),
@@ -406,24 +434,21 @@
             pltpu.VMEM((xdev, ydev), BF16),
             pltpu.VMEM((xdev, ydev), F32),
             pltpu.VMEM((zdev, xdev, ydev), F32),
+            pltpu.VMEM((3, centers.shape[0], PACK, ydev), F32),
             pltpu.VMEM((zdev, xdev, ydev), F32),
             pltpu.VMEM((centers.shape[0], zdev, xdev, ydev), F32),
             pltpu.VMEM((xdev, ydev), F32),
             pltpu.VMEM((xdev, ydev), F32),
             pltpu.VMEM((xdev, ydev), F32),
             pltpu.VMEM((ndepth, rows_out, ydev), F32),
-            pltpu.VMEM((ndepth, 3, rows_out, ydev), jnp.int16),
-            pltpu.VMEM((ndepth, 3, rows_out, ydev), jnp.int16),
+            pltpu.VMEM((ndepth, 3 * max(PACK, rows_out) + PACK, ydev), jnp.int16),
+            pltpu.VMEM((ndepth, 3 * max(PACK, rows_out) + PACK, ydev), jnp.int16),
             pltpu.VMEM((3, unit, ydev), F32),
             pltpu.VMEM((3, rows_out, ydev), F32),
-            pltpu.VMEM((ndepth, SUB, ydev), F32),
-            pltpu.VMEM((ndepth, SUB, ydev), F32),
             dma((6,)),
             dma((PIECES,)),
-            dma((6,)),
-            dma((6,)),
-            dma((ndepth,)),
-            dma((ndepth,)),
+            dma((4 * units + 2,)),
+            dma((4 * units + 2,)),
             dma((ndepth,)),
             dma((ndepth,)),
             dma((ndepth,)),
@@ -431,6 +456,13 @@
         ],
         compiler_params=pltpu.CompilerParams(collective_id=0, has_side_effects=True),
     )(field, brick_live, order, centers, widths, heights, colours)
+    return pl.pallas_call(
+        hand_over,
+        out_shape=tuple(jax.ShapeDtypeStruct(part.shape, F32) for part in done),
+        in_specs=[vmem] * 2,
+        out_specs=(pl.BlockSpec(memory_space=pl.ANY),) * 2,
+        scratch_shapes=[dma((2,))],
+    )(*(pltpu.with_memory_space_constraint(part, pltpu.VMEM) for part in done))
 
 
 def solution(mesh):

time: 15.5 us -> 14.9 us (0.961)
  local copies, waits for them, and re-layouts: 1.23 us -> 0 us
  Pallas kernels: 13.4 us -> 14 us
    unnamed x2 -> x0, local copies, waits for them, and re-layouts: 1.23 us -> none
    pallas_call x0 -> x1, Pallas kernels: none -> 0.64 us  [local(): pl.pallas_call(hand_over, out_shape=tuple((jax.ShapeDtypeStruct(part.shap...]
where the time goes in v2:
time: 14.9 us; the launch traced here: 14.7 us
  Pallas kernels  14 us (94%)
  between operations  0.64 us (4%)
    pallas_call x1, Pallas kernels, local(): pl.pallas_call(functools.partial(kernel, counts, step_len), out_shape=(pl...  13.4 us
    pallas_call x1, Pallas kernels, local(): pl.pallas_call(hand_over, out_shape=tuple((jax.ShapeDtypeStruct(part.shap...  0.64 us

profile of v2, /device:TPU:0, one launch (start us, length us, event | category | flops | bytes accessed | tf_op | source)
XLA Modules:
  0.0 14.7 jit_solution(5907349788125226985)
XLA Ops:
  0.6 13.4 %shard_map.86 = (f32[3,32,128]{2,1,0:T(8,128)S(1)}, f32[32,128]{1,0:T(8,128)S(1)}) custom-call(bf16[32,128,128]{2,1,0:T(8,128)(2,1)} %field.1, s32[1,4,4]{2,1,0:T(4,128)} %live_in.1, s32[16,16]{1,0:T(8,128)} %order_in.1, f32[4]{0:T(128)} %centers_in.1, f32[4]{0:T(128)} %widths_in.1, f32[4]{0:T(128)} %heights_in.1, f32[4,3]{1,0:T(4,128)} %colours_in.1), custom_call_target="tpu_custom_call" | custom-call | tf_op jit(solution)/shard_map/pallas_call | solution.py:411
  14.0 0.6 %shard_map.87 = (f32[3,32,128]{2,1,0:T(8,128)}, f32[32,128]{1,0:T(8,128)}) custom-call(f32[3,32,128]{2,1,0:T(8,128)S(1)} %get-tuple-element.4.colour, f32[32,128]{1,0:T(8,128)S(1)} %get-tuple-element.5.logt), custom_call_target="tpu_custom_call" | custom-call | tf_op jit(solution)/shard_map/pallas_call | solution.py:459
